TPU v7x, 32 devices: a whole 2x2x4 slice. The times are simulated.
32 devices in a mesh: row: 4 (over y, x), col: 8 (over z, core).
Axes of the slice: x: 2, y: 2, z: 4, core: 2. Of those that a mesh axis runs over, the one named last changes fastest.
Arguments:
- cam_jac: bfloat16 [2, 2, 6, 512, 1024], P(None, None, None, ('row', 'col')), may hold values from -0.09375 to 0.09375
- pt_jac: bfloat16 [2, 2, 3, 512, 1024], P(None, None, None, ('row', 'col')), may hold values from -6 to 6
- resid: bfloat16 [2, 2, 512, 1024], P(None, None, ('row', 'col')), may hold values from -6 to 6
- partner: int32 [512, 1024], P(('row', 'col')), may hold values from 0 to 511, as said below
- count: int32 [512], P(('row', 'col')), may hold values from 512 to 1024
- tile_map: int32 [512], replicated, may hold values from 0 to 511, as said below
Outputs:
- coupling: bfloat16 [6, 6, 512, 512], P(None, None, 'row', 'col')
- camera_update: float32 [6, 512], P(None, 'row')
- residual: float32 [6, 512], P(None, 'row')
Inputs may be any that keep to these rules, and one draw needn't show every extreme that they name: partner[a, t] is never a. `tile_map`: a permutation of the tile positions; of the 16 consecutive scenes of each device, exactly 4 have positions in each block of 128 consecutive positions.
All inputs are finite; a program needn't handle non-finite values.
Results may differ from a plain program's by a relative error of at most 0.0015.
Values may be sent and summed in bfloat16 or wider, within the bound.
A program may use at most 64 MiB of HBM per device.

v0:
```python
import jax
import jax.numpy as jnp
from jax import lax
from jax.sharding import PartitionSpec as P

ITERS = 3


CAMERA_DAMPING = 1.0
POINT_DAMPING = 1.0


def cross_product(first_vec, second_vec):
    return jnp.stack(
        [
            first_vec[1] * second_vec[2] - first_vec[2] * second_vec[1],
            first_vec[2] * second_vec[0] - first_vec[0] * second_vec[2],
            first_vec[0] * second_vec[1] - first_vec[1] * second_vec[0],
        ],
        axis=0,
    )


def point_terms(camera, points_jac, errors):
    camera = camera.astype(jnp.float32)
    points_jac = points_jac.astype(jnp.float32)
    errors = errors.astype(jnp.float32)
    own_jac, other_jac = (camera[0], camera[1])
    own_point, other_point = (points_jac[0], points_jac[1])
    own_error, other_error = (errors[0], errors[1])
    point_hessian = jnp.sum(own_point[:, :, None] * own_point[:, None, :], axis=0)
    point_hessian = point_hessian + jnp.sum(
        other_point[:, :, None] * other_point[:, None, :], axis=0
    )
    point_hessian = point_hessian + POINT_DAMPING * jnp.eye(3, dtype=jnp.float32)[:, :, None, None]
    first_row, second_row, third_row = (point_hessian[0], point_hessian[1], point_hessian[2])
    cofactor_first = cross_product(second_row, third_row)
    cofactor_second = cross_product(third_row, first_row)
    cofactor_third = cross_product(first_row, second_row)
    determinant = jnp.sum(first_row * cofactor_first, axis=0)
    inverse = jnp.stack([cofactor_first, cofactor_second, cofactor_third], axis=1) / determinant
    w_own = jnp.sum(own_jac[:, :, None] * own_point[:, None, :], axis=0)
    w_other = jnp.sum(other_jac[:, :, None] * other_point[:, None, :], axis=0)
    point_rhs = -(
        jnp.sum(own_point * own_error[:, None], axis=0)
        + jnp.sum(other_point * other_error[:, None], axis=0)
    )
    own_vi = jnp.sum(w_own[:, :, None] * inverse[None, :, :], axis=1)
    other_vi = jnp.sum(w_other[:, :, None] * inverse[None, :, :], axis=1)
    diag_own = jnp.sum(own_jac[:, :, None] * own_jac[:, None, :], axis=0) - jnp.sum(
        own_vi[:, None, :] * w_own[None, :, :], axis=2
    )
    diag_other = jnp.sum(other_jac[:, :, None] * other_jac[:, None, :], axis=0) - jnp.sum(
        other_vi[:, None, :] * w_other[None, :, :], axis=2
    )
    link = -jnp.sum(own_vi[:, None, :] * w_other[None, :, :], axis=2)
    grad_own = -jnp.sum(own_jac * own_error[:, None], axis=0) - jnp.sum(
        own_vi * point_rhs[None], axis=1
    )
    grad_other = -jnp.sum(other_jac * other_error[:, None], axis=0) - jnp.sum(
        other_vi * point_rhs[None], axis=1
    )
    return (diag_own, diag_other, link, grad_own, grad_other)


def conjugate_steps(right_side, apply_operator, inner_product):
    solution = jnp.zeros_like(right_side)
    remainder = right_side
    direction = right_side
    norm_now = inner_product(remainder, remainder)
    for iteration in range(ITERS):
        product_vec = apply_operator(direction)
        step_size = norm_now / inner_product(direction, product_vec)
        solution = solution + step_size * direction
        remainder = remainder - step_size * product_vec
        norm_next = inner_product(remainder, remainder)
        direction = remainder + norm_next / norm_now * direction
        norm_now = norm_next
    return (solution, remainder)


def shards(cam_jac, pt_jac, resid, partner, count, tile_map):
    row_count = lax.axis_size("row")
    col_count = lax.axis_size("col")
    scenes = tile_map.shape[0]
    scn_local = partner.shape[0]
    points = partner.shape[1]
    tile_rows = scenes // row_count
    tile_cols = scenes // col_count
    per_group = scn_local // row_count
    row_index = lax.axis_index("row")
    col_index = lax.axis_index("col")
    device = row_index * col_count + col_index
    positions = jnp.arange(scenes, dtype=jnp.int32)
    tile_own = lax.dynamic_slice_in_dim(tile_map, device * scn_local, scn_local)
    local_rank = jnp.sum((tile_own[None, :] < tile_own[:, None]).astype(jnp.int32), axis=1)
    active = (jnp.arange(points, dtype=jnp.int32)[None, :] < count[:, None]).astype(jnp.float32)
    diag_own, diag_other, link, grad_own, grad_other = point_terms(cam_jac, pt_jac, resid)
    values = (
        jnp.concatenate(
            [
                link.reshape(36, scn_local, points),
                diag_other.reshape(36, scn_local, points),
                grad_other,
            ],
            axis=0,
        )
        * active[None]
    )
    values = jnp.moveaxis(values, 1, 0)

    def scene_sums(item):
        scene_values, scene_partner = item
        hits = scene_partner[:, None] == positions[None, :]
        tile_other = jnp.sum(jnp.where(hits, tile_map[None, :], 0), axis=1)
        onehot = (tile_other[:, None] == positions[None, :]).astype(jnp.float32)
        return jnp.dot(
            scene_values,
            onehot,
            precision=lax.Precision.HIGHEST,
            preferred_element_type=jnp.float32,
        )

    per_scene = lax.map(scene_sums, (values, partner))
    link_rows = per_scene[:, :36, :]
    other_sum = jnp.sum(per_scene[:, 36:, :], axis=0)
    ordering = (local_rank[None, :] == jnp.arange(scn_local, dtype=jnp.int32)[:, None]).astype(
        jnp.float32
    )
    panel = jnp.einsum("rs,sxc->xrc", ordering, link_rows, precision=lax.Precision.HIGHEST)
    panel = panel.reshape(36, row_count, per_group, col_count, tile_cols).transpose(0, 1, 3, 2, 4)
    panel_short = panel.astype(jnp.bfloat16)
    own_onehot = (tile_own[:, None] == positions[None, :]).astype(jnp.float32)
    own_diag = jnp.sum(diag_own * active, axis=-1).reshape(36, scn_local)
    own_grad = jnp.sum(grad_own * active, axis=-1)
    own_both = jnp.concatenate([own_diag, own_grad], axis=0)
    own_spread = jnp.dot(
        own_both, own_onehot, precision=lax.Precision.HIGHEST, preferred_element_type=jnp.float32
    )
    both_part = own_spread + other_sum
    diag_part = both_part[:36]
    grad_part = both_part[36:]
    shaped = panel_short.reshape(36, row_count * col_count, per_group, tile_cols)
    received = lax.all_to_all(shaped, ("row", "col"), split_axis=1, concat_axis=1, tiled=True)
    received = received.reshape(36, tile_rows, tile_cols)
    diag_all, grad_all = lax.psum((diag_part, grad_part), ("row", "col"))
    row_start = row_index * tile_rows
    col_start = col_index * tile_cols
    devices = scenes // scn_local
    tiles_grid = tile_map.reshape(devices, scn_local)
    inblock = (tiles_grid >= row_start) & (tiles_grid < row_start + tile_rows)
    lower = (tiles_grid[:, None, :] < tiles_grid[:, :, None]) & inblock[:, None, :]
    within_all = jnp.sum(lower.astype(jnp.int32), axis=2)
    slot_from = (jnp.arange(devices, dtype=jnp.int32)[:, None] * per_group + within_all).reshape(-1)
    slot_to = (tiles_grid - row_start).reshape(-1)
    slots = jnp.arange(tile_rows, dtype=jnp.int32)
    to_table = ((slot_to[:, None] == slots[None, :]) & inblock.reshape(-1)[:, None]).astype(
        jnp.bfloat16
    )
    from_table = (slot_from[:, None] == slots[None, :]).astype(jnp.bfloat16)
    selection = jnp.dot(to_table.T, from_table, preferred_element_type=jnp.float32).astype(
        jnp.bfloat16
    )
    coupling_tile = jnp.einsum(
        "pk,xkc->xpc", selection, received, preferred_element_type=jnp.float32
    )
    coupling_tile = coupling_tile.astype(jnp.bfloat16).reshape(6, 6, tile_rows, tile_cols)
    coupling_wide = coupling_tile.astype(jnp.float32)
    zero_at = row_index * 0

    def tile_products(rows_part, cols_part):
        forward = jnp.einsum(
            "xyij,yj->xi", coupling_wide, cols_part, precision=lax.Precision.HIGHEST
        )
        backward = jnp.einsum(
            "xyij,xi->yj", coupling_wide, rows_part, precision=lax.Precision.HIGHEST
        )
        empty = jnp.zeros((6, scenes), jnp.float32)
        spread = lax.dynamic_update_slice(empty, forward, (zero_at, row_start))
        spread = spread + lax.dynamic_update_slice(empty, backward, (zero_at, col_start))
        return lax.psum(spread, ("row", "col"))

    diag_blocks = diag_all.reshape(6, 6, scenes)

    def apply_full(direction):
        rows_part = lax.dynamic_slice_in_dim(direction, row_start, tile_rows, 1)
        cols_part = lax.dynamic_slice_in_dim(direction, col_start, tile_cols, 1)
        summed = tile_products(rows_part, cols_part)
        result = CAMERA_DAMPING * direction
        result = result + jnp.einsum(
            "xyi,yi->xi", diag_blocks, direction, precision=lax.Precision.HIGHEST
        )
        return result + summed

    def inner_full(first_vec, second_vec):
        return jnp.sum(first_vec * second_vec)

    whole_solution, whole_remainder = conjugate_steps(grad_all, apply_full, inner_full)
    solution = lax.dynamic_slice_in_dim(whole_solution, row_start, tile_rows, 1)
    remainder = lax.dynamic_slice_in_dim(whole_remainder, row_start, tile_rows, 1)
    return (coupling_tile, solution, remainder)


def solution(mesh):
    return jax.shard_map(
        shards,
        mesh=mesh,
        in_specs=(
            P(None, None, None, ("row", "col"), None),
            P(None, None, None, ("row", "col"), None),
            P(None, None, ("row", "col"), None),
            P(("row", "col"), None),
            P(("row", "col")),
            P(),
        ),
        out_specs=(P(None, None, "row", "col"), P(None, "row"), P(None, "row")),
        check_vma=False,
    )
```

profile of v0, /device:TPU:0, one launch (start us, length us, event | category | flops | bytes accessed | tf_op | source)
XLA Modules:
  0.0 395.3 jit_solution(5437719041077850212)
XLA Ops:
  13.1 2.9 multiply_reduce_fusion.8
  16.1 2.6 multiply_reduce_fusion.3
  23.3 6.3 %multiply_reduce_fusion = (f32[6,6,16,1024]{3,2,1,0:T(8,128)}, f32[6,6,16,1024]{3,2,1,0:T(8,128)}, f32[6,6,16,1024]{3,2,1,0:T(8,128)}) fusion(f32[6,3,16,1024]{3,2,1,0:T(8,128)S(1)} %copy-done.1, f32[6,3,16,1024]{3,2,1,0:T(8,128)S(1)} %get-tuple-element.89, f32[6,3,16,1024]{3,2,1,0:T(8,128)S(1)} %get-tuple-element.127, ...), kind=kLoop, calls=%fused_computation.11 | loop fusion | flops 8847360 | bytes 11796480 | tf_op jit(solution)/shard_map/reduce_sum | solution.py:50
  30.8 2.0 neg.20
  35.0 2.8 sub.170
  37.8 2.8 fusion.6
  40.6 78.3 %while.12 = (s32[]{:T(128)}, f32[16,78,512]{2,1,0:T(8,128)}, f32[16,78,1024]{2,0,1:T(8,128)}, s32[16,1024]{1,0:T(8,128)}, s32[512]{0:T(512)S(1)}, /*index=5*/s32[]{:T(128)}) while((s32[]{:T(128)}, f32[16,78,512]{2,1,0:T(8,128)}, f32[16,78,1024]{2,0,1:T(8,128)}, s32[16,1024]{1,0:T(8,128)}, s32[512]{0:T(512)S(1)}, ...), condition=%wide.region_16.0_spmd.clone.clone, body=%wide.region_14.16_spmd.clone.clone.sunk | while | flops 492829696 | bytes 1144921 | solution.py:124
  41.9 2.0 constant_dynamic-slice_fusion.5
  46.8 2.0 constant_dynamic-slice_fusion.5
  51.6 2.0 constant_dynamic-slice_fusion.5
  56.5 2.0 constant_dynamic-slice_fusion.5
  61.4 2.0 constant_dynamic-slice_fusion.5
  66.3 2.0 constant_dynamic-slice_fusion.5
  81.0 2.0 constant_dynamic-slice_fusion.5
  90.8 2.0 constant_dynamic-slice_fusion.5
  95.7 2.0 constant_dynamic-slice_fusion.5
  105.5 2.0 constant_dynamic-slice_fusion.5
  121.8 2.7 fusion.12
  127.4 7.3 %all-to-all-start = ((bf16[32,2,4608]{2,1,0:T(2,128)(2,1)}), bf16[32,2,4608]{2,1,0:T(2,128)(2,1)S(1)}, u32[]{:S(2)}, u32[]{:S(2)}) async-start(bf16[32,2,4608]{2,1,0:T(2,128)(2,1)} %reshape.571), calls=%async_computation | async-start | bytes 1179648 | tf_op jit(solution)/shard_map/all_to_all | solution.py:144
  135.0 41.1 %psum.35 = f32[6,512]{1,0:T(8,128)S(1)} all-reduce(f32[6,512]{1,0:T(8,128)S(1)} %slice.143), channel_id=1, replica_groups=mesh['row'=4,'col'=8] {'row','col'}, use_global_device_ids=true, to_apply=%region_26.27 | all-reduce | flops 3072 | bytes 24576 | tf_op jit(solution)/shard_map/psum | solution.py:146
  176.4 71.8 %all-reduce.2.cloned.1.call-done = f32[6,6,512]{2,1,0:T(8,128)} async-done(((f32[6,6,512]{2,1,0:T(8,128)}), f32[6,6,512]{2,1,0:T(8,128)}) %all-reduce.2.cloned.1.call-update) | async-done | bytes 73744 | tf_op jit(solution)/shard_map/psum | solution.py:146
  252.8 41.2 %psum.37 = f32[6,512]{1,0:T(8,128)S(1)} all-reduce(f32[6,512]{1,0:T(8,128)S(1)} %add.132), channel_id=1, replica_groups=mesh['row'=4,'col'=8] {'row','col'}, use_global_device_ids=true, to_apply=%region_29.30 | all-reduce | flops 3072 | bytes 24576 | tf_op jit(solution)/shard_map/psum | solution.py:181
  299.6 40.0 %psum.38 = f32[6,512]{1,0:T(8,128)S(1)} all-reduce(f32[6,512]{1,0:T(8,128)S(1)} %add.136), channel_id=1, replica_groups=mesh['row'=4,'col'=8] {'row','col'}, use_global_device_ids=true, to_apply=%region_32.33 | all-reduce | flops 3072 | bytes 24576 | tf_op jit(solution)/shard_map/psum | solution.py:181
  345.2 40.1 %psum.39 = f32[6,512]{1,0:T(8,128)S(1)} all-reduce(f32[6,512]{1,0:T(8,128)S(1)} %add.141), channel_id=1, replica_groups=mesh['row'=4,'col'=8] {'row','col'}, use_global_device_ids=true, to_apply=%region_35.36 | all-reduce | flops 3072 | bytes 24576 | tf_op jit(solution)/shard_map/psum | solution.py:181
  (172 shorter events, 90.0 us)
Async XLA Ops:
  7.2 241.0 %all-reduce.2.cloned.1.call-start = ((), (), s32[]{:S(2)}) async-start(), calls=%async_computation.1 | async-start | bytes 196608 | tf_op jit(solution)/shard_map/psum | solution.py:146
  8.4 0.7 copy-start.4
  8.4 0.9 copy-start.5
  8.6 2.1 copy-start.10
  8.6 2.1 copy-start.9
  16.1 2.6 copy-start.12
  18.7 3.9 copy-start.1
  29.6 1.0 copy-start.7
  30.8 2.4 copy-start.2
  30.8 3.1 copy-start.3
  33.9 0.7 copy-start.11
  33.9 1.0 copy-start.6
  127.4 121.7 %all-to-all-start = ((bf16[32,2,4608]{2,1,0:T(2,128)(2,1)}), bf16[32,2,4608]{2,1,0:T(2,128)(2,1)S(1)}, u32[]{:S(2)}, u32[]{:S(2)}) async-start(bf16[32,2,4608]{2,1,0:T(2,128)(2,1)} %reshape.571), calls=%async_computation | async-start | bytes 1179648 | tf_op jit(solution)/shard_map/all_to_all | solution.py:144
  250.5 89.1 %copy-start.8 = (f32[6,6,512]{2,1,0:T(8,128)S(1)}, f32[6,6,512]{2,1,0:T(8,128)}, u32[]{:S(2)}) copy-start(f32[6,6,512]{2,1,0:T(8,128)} %all-reduce.2.cloned.1.call-done) | copy-start | bytes 221188
  251.3 137.2 %copy-start = (bf16[36,64,128]{2,1,0:T(8,128)(2,1)}, bf16[36,64,128]{2,1,0:T(8,128)(2,1)S(1)}, u32[]{:S(2)}) copy-start(bf16[36,64,128]{2,1,0:T(8,128)(2,1)S(1)} %convolution_convert_fusion) | copy-start | bytes 1769476
Sparse Core Ops, SparseCore 0:
  121.7 126.4 all-reduce.1
where the time goes:
time: 398 us; the launch traced here: 395 us
  blocking collectives  162 us (41%)
  waiting for transfers between devices  71.8 us (18%)
  local copies, waits for them, and re-layouts  53.9 us (14%)
  other arithmetic  44.9 us (11%)
  matrix products  33.6 us (8%)
  between operations  21.2 us (5%)
  starting transfers between devices  7.36 us (2%)
    psum x3, blocking collectives, tile_products(): return lax.psum(spread, ('row', 'col'))  121 us
    psum x1, waiting for transfers between devices, shards(): diag_all, grad_all = lax.psum((diag_part, grad_part), ('row', 'col'))  71.8 us
    dynamic_slice x32, local copies, waits for them, and re-layouts, shards(): per_scene = lax.map(scene_sums, (values, partner))  44.5 us
    psum x1, blocking collectives, shards(): diag_all, grad_all = lax.psum((diag_part, grad_part), ('row', 'col'))  41.1 us
    dot_general x16, matrix products, scene_sums(): jnp.dot(scene_values, onehot, precision=lax.Precision.HIGHEST, preferred_...  26.2 us
  transfers between devices with their start and end apart: 2, of which 1 were waited for; matrix products, arithmetic and copies ran while one was open for 2% of the time, Pallas kernels for 0%

commit v1 on v0

v1 whole, which is shorter than its diff:
```python
import functools

import jax
import jax.numpy as jnp
from jax import lax
from jax.experimental import pallas as pl
from jax.experimental.pallas import tpu as pltpu
from jax.sharding import PartitionSpec as P

ITERS = 3
CAMERA_DAMPING = 1.0
POINT_DAMPING = 1.0
LANES = 128
OTHER_ROWS = 64
OWN_ROWS = 32
ROWS = OTHER_ROWS + OWN_ROWS
PAIRS = [(x, y) for x in range(6) for y in range(x, 6)]
SPARE = [y * 8 + 6 + h for y in range(6) for h in range(2)] + list(range(48, 63))
NT = (((1,), (1,)), ((), ()))
MESH = pl.DeviceIdType.MESH
VMEM_LIMIT = 60 * 1024 * 1024


def total_of(terms):
    result = terms[0]
    for term in terms[1:]:
        result = result + term
    return result


def point_rows(cam, pt, err):
    hess = {}
    for i in range(3):
        for j in range(i, 3):
            value = total_of([pt[s][r][i] * pt[s][r][j] for s in range(2) for r in range(2)])
            hess[i, j] = value + POINT_DAMPING if i == j else value
    a, b, c = hess[0, 0], hess[0, 1], hess[0, 2]
    d, e, f = hess[1, 1], hess[1, 2], hess[2, 2]
    cof = {
        (0, 0): d * f - e * e,
        (0, 1): e * c - b * f,
        (0, 2): b * e - d * c,
        (1, 1): f * a - c * c,
        (1, 2): c * b - a * e,
        (2, 2): a * d - b * b,
    }
    scale = 1.0 / (a * cof[0, 0] + b * cof[0, 1] + c * cof[0, 2])
    inv = {key: value * scale for key, value in cof.items()}
    rhs = [-total_of([pt[s][r][i] * err[s][r] for s in range(2) for r in range(2)]) for i in range(3)]
    w = [
        [[total_of([cam[s][r][x] * pt[s][r][i] for r in range(2)]) for i in range(3)] for x in range(6)]
        for s in range(2)
    ]
    wv = [
        [
            [total_of([w[s][x][i] * inv[min(i, j), max(i, j)] for i in range(3)]) for j in range(3)]
            for x in range(6)
        ]
        for s in range(2)
    ]
    link = {
        (x, y): -total_of([wv[0][x][j] * w[1][y][j] for j in range(3)])
        for x in range(6)
        for y in range(6)
    }
    sides = []
    for s in range(2):
        rows = [
            total_of([cam[s][r][x] * cam[s][r][y] for r in range(2)])
            - total_of([wv[s][x][j] * w[s][y][j] for j in range(3)])
            for x, y in PAIRS
        ]
        rows += [
            -total_of([cam[s][r][x] * err[s][r] for r in range(2)])
            - total_of([wv[s][x][j] * rhs[j] for j in range(3)])
            for x in range(6)
        ]
        sides.append(rows)
    return link, sides[0], sides[1]


def assemble_kernel(
    nrow, ncol, cam_ref, pt_ref, err_ref, partner_ref, count_ref, map_ref, target_ref,
    mat_ref, diag_ref, grad_ref, panel_ref, vals, live_partner, acc,
):
    scn, points = partner_ref.shape
    scenes = map_ref.shape[1]
    blocks = points // LANES
    base = (lax.axis_index("row") * ncol + lax.axis_index("col")) * scn

    def point_block(jb, carry):
        lanes = pl.ds(pl.multiple_of(jb * LANES, LANES), LANES)
        take = lambda ref, *at: ref[at + (slice(None), lanes)].astype(jnp.float32)
        cam = [[[take(cam_ref, s, r, x) for x in range(6)] for r in range(2)] for s in range(2)]
        pt = [[[take(pt_ref, s, r, x) for x in range(3)] for r in range(2)] for s in range(2)]
        err = [[take(err_ref, s, r) for r in range(2)] for s in range(2)]
        slot = lax.broadcasted_iota(jnp.int32, (scn, LANES), 1) + jb * LANES
        active = slot < count_ref[...]
        live_partner[:, lanes] = jnp.where(active, partner_ref[:, lanes], -1)
        link, own, other = point_rows(cam, pt, err)

        def put(row, value):
            vals[pl.ds(jb * (scn * ROWS) + row, scn, stride=ROWS), :] = value

        zero = jnp.zeros((scn, LANES), jnp.float32)
        for (x, y), value in link.items():
            put(y * 8 + x, value)
        for u in range(27):
            put(SPARE[u], other[u])
            put(OTHER_ROWS + u, jnp.where(active, own[u], 0.0))
        put(OTHER_ROWS - 1, zero)
        for u in range(27, OWN_ROWS):
            put(OTHER_ROWS + u, zero)
        return carry

    lax.fori_loop(0, blocks, point_block, 0)
    acc[...] = jnp.zeros_like(acc)
    chunk = 256
    low = lax.broadcasted_iota(jnp.int32, (8, chunk), 0) < 6

    def scene(s, own_sum):
        start = lambda jb: pl.multiple_of((jb * scn + s) * ROWS, 8)
        full = jnp.concatenate([vals[pl.ds(start(jb), OTHER_ROWS), :] for jb in range(blocks)], axis=1)
        high = full.astype(jnp.bfloat16)
        rest = (full - high.astype(jnp.float32)).astype(jnp.bfloat16)
        both = jnp.concatenate([high, rest], axis=0)
        ids = live_partner[pl.ds(s, 1), :]
        for b in range(scenes // chunk):
            spot = lax.broadcasted_iota(jnp.int32, (chunk, points), 0) + b * chunk
            onehot = jnp.where(spot == ids, 1.0, 0.0).astype(jnp.bfloat16)
            sums = lax.dot_general(both, onehot, NT, preferred_element_type=jnp.float32)
            sums = sums[:OTHER_ROWS] + sums[OTHER_ROWS:]
            cols = slice(b * chunk, (b + 1) * chunk)
            acc[:, cols] += sums
            for y in range(6):
                part = jnp.where(low, sums[y * 8 : y * 8 + 8], 0.0)
                mat_ref[pl.ds(pl.multiple_of(s * 8, 8), 8), y * scenes + b * chunk : y * scenes + (b + 1) * chunk] = (
                    part.astype(jnp.bfloat16).astype(jnp.float32)
                )
        own = total_of([vals[pl.ds(start(jb) + OTHER_ROWS, OWN_ROWS), :] for jb in range(blocks)])
        own = jnp.sum(own, axis=1, keepdims=True)
        here = lax.broadcasted_iota(jnp.int32, (OWN_ROWS, scenes), 1) == base + s
        return own_sum + jnp.where(here, own, 0.0)

    own_sum = lax.fori_loop(0, scn, scene, jnp.zeros((OWN_ROWS, scenes), jnp.float32))
    diag_ref[...] = jnp.zeros_like(diag_ref)
    grad_ref[...] = jnp.zeros_like(grad_ref)
    for u in range(27):
        row = acc[SPARE[u] : SPARE[u] + 1, :] + own_sum[u : u + 1, :]
        if u < 21:
            x, y = PAIRS[u]
            diag_ref[y * 8 + x : y * 8 + x + 1, :] = row
            if x != y:
                diag_ref[x * 8 + y : x * 8 + y + 1, :] = row
        else:
            grad_ref[u - 21 : u - 20, :] = row

    rows = panel_ref.shape[1]
    order = jnp.where(
        lax.broadcasted_iota(jnp.int32, (nrow * rows, scn * 8), 0) == target_ref[...], 1.0, 0.0
    ).astype(jnp.bfloat16)
    spots = jnp.where(
        lax.broadcasted_iota(jnp.int32, (scenes, scenes), 0) == map_ref[...], 1.0, 0.0
    ).astype(jnp.bfloat16)
    width = scenes // ncol
    ordered = []
    for y in range(6):
        piece = mat_ref[:, y * scenes : (y + 1) * scenes].astype(jnp.bfloat16)
        piece = jnp.dot(order, piece, preferred_element_type=jnp.float32).astype(jnp.bfloat16)
        ordered.append(lax.dot_general(piece, spots, NT, preferred_element_type=jnp.float32))
    for c in range(ncol):
        wide = jnp.concatenate([o[:, c * width : (c + 1) * width] for o in ordered], axis=1)
        for r in range(nrow):
            panel_ref[r * ncol + c] = wide[r * rows : (r + 1) * rows].astype(jnp.bfloat16)


def iterate_kernel(
    nrow, ncol, scn, mat_ref, diag_ref, grad_ref, panel_ref, recv_ref, sol_ref, res_ref,
    buf_col, buf_row, send_p, recv_p, send_c, recv_c, send_r, recv_r,
):
    row, col = lax.axis_index("row"), lax.axis_index("col")
    count = nrow * ncol
    me = row * ncol + col
    base = me * scn
    scenes = grad_ref.shape[1]

    barrier = pltpu.get_barrier_semaphore()

    def greet(off, carry):
        peer = lax.rem(me + off, count)
        pl.semaphore_signal(barrier, inc=1, device_id=(peer // ncol, lax.rem(peer, ncol)), device_id_type=MESH)
        return carry

    lax.fori_loop(1, count, greet, 0)
    pl.semaphore_wait(barrier, count - 1)

    def panel_copy(off):
        peer = lax.rem(me + off, count)
        return pltpu.make_async_remote_copy(
            src_ref=panel_ref.at[peer],
            dst_ref=recv_ref.at[me],
            send_sem=send_p.at[off],
            recv_sem=recv_p.at[off],
            device_id=(peer // ncol, lax.rem(peer, ncol)),
            device_id_type=MESH,
        )

    def gathered(value, buf, spot, turn, size, send, recv, device_of, between=None):
        buf[turn, spot] = value
        copies = []
        for off in range(1, size):
            copy = pltpu.make_async_remote_copy(
                src_ref=buf.at[turn, spot],
                dst_ref=buf.at[turn, spot],
                send_sem=send.at[turn, off],
                recv_sem=recv.at[turn, off],
                device_id=device_of(lax.rem(spot + off, size)),
                device_id_type=MESH,
            )
            copy.start()
            copies.append(copy)
        if between is not None:
            between()
        for copy in copies:
            copy.wait()
        return total_of([buf[turn, i] for i in range(size)])

    def all_sum(value, turn, between=None):
        value = gathered(value, buf_col, col, turn, ncol, send_c, recv_c, lambda p: (row, p), between)
        return gathered(value, buf_row, row, turn, nrow, send_r, recv_r, lambda p: (p, col))

    def start_panels():
        def step(off, carry):
            panel_copy(off).start()
            return carry

        lax.fori_loop(1, count, step, 0)
        recv_ref[me] = panel_ref[me]

    lane = lax.broadcasted_iota(jnp.int32, (8, scenes), 1)

    def local_product(vector):
        flat = jnp.concatenate([vector[y : y + 1] for y in range(6)], axis=1)

        def step(s, carry):
            back, out = carry
            here = lane == base + s
            own = jnp.sum(jnp.where(here, vector, 0.0), axis=1, keepdims=True)
            part = mat_ref[pl.ds(pl.multiple_of(s * 8, 8), 8), :]
            ahead = jnp.sum(part * flat, axis=1, keepdims=True)
            return back + part * own, out + jnp.where(here, ahead, 0.0)

        zero = jnp.zeros((8, scenes), jnp.float32)
        back, out = lax.fori_loop(0, scn, step, (jnp.zeros((8, 6 * scenes), jnp.float32), zero))
        back = jnp.sum(back, axis=0, keepdims=True)
        for y in range(6):
            out = out + diag_ref[y * 8 : y * 8 + 8, :] * vector[y : y + 1]
        back = jnp.concatenate(
            [back[:, y * scenes : (y + 1) * scenes] for y in range(6)]
            + [jnp.zeros((2, scenes), jnp.float32)],
            axis=0,
        )
        return out + back

    def inner(first, second):
        return jnp.sum(jnp.sum(first * second, axis=1, keepdims=True), axis=0, keepdims=True)

    remainder = all_sum(grad_ref[...], 0, start_panels)
    result = jnp.zeros_like(remainder)
    direction = remainder
    norm_now = inner(remainder, remainder)
    for turn in range(ITERS):
        image = CAMERA_DAMPING * direction + all_sum(local_product(direction), turn + 1)
        size = norm_now / inner(direction, image)
        result = result + size * direction
        remainder = remainder - size * image
        norm_next = inner(remainder, remainder)
        direction = remainder + norm_next / norm_now * direction
        norm_now = norm_next
    sol_ref[...] = result
    res_ref[...] = remainder

    def finish(off, carry):
        panel_copy(off).wait()
        return carry

    lax.fori_loop(1, count, finish, 0)


def place_kernel(recv_ref, place_ref, map_ref, sol_ref, res_ref, coupling_ref, update_ref, residual_ref):
    tile_rows, width = coupling_ref.shape[2:]
    held = recv_ref.shape[0]
    for x in range(6):
        spot = lax.broadcasted_iota(jnp.int32, (tile_rows, held), 0) + x * tile_rows
        chosen = jnp.where(spot == place_ref[...], 1.0, 0.0).astype(jnp.bfloat16)
        block = jnp.dot(chosen, recv_ref[...], preferred_element_type=jnp.float32).astype(jnp.bfloat16)
        for y in range(6):
            coupling_ref[x, y] = block[:, y * width : (y + 1) * width]
    scenes = map_ref.shape[1]
    spot = lax.broadcasted_iota(jnp.int32, (tile_rows, scenes), 0) + lax.axis_index("row") * tile_rows
    chosen = jnp.where(spot == map_ref[...], 1.0, 0.0).astype(jnp.bfloat16)
    for source, target in ((sol_ref, update_ref), (res_ref, residual_ref)):
        left = source[...]
        moved = None
        for unused in range(3):
            short = left.astype(jnp.bfloat16)
            left = left - short.astype(jnp.float32)
            part = lax.dot_general(short, chosen, NT, preferred_element_type=jnp.float32)
            moved = part if moved is None else moved + part
        target[...] = moved[:6]


def shards(cam_jac, pt_jac, resid, partner, count, tile_map):
    nrow = lax.axis_size("row")
    ncol = lax.axis_size("col")
    scenes = tile_map.shape[0]
    scn, points = partner.shape
    devices = nrow * ncol
    tile_rows = scenes // nrow
    width = scenes // ncol
    group = scn // nrow
    rows = -(-6 * group // 8) * 8
    row_index = lax.axis_index("row")
    device = row_index * ncol + lax.axis_index("col")
    tiles = tile_map.reshape(devices, scn)
    rank = jnp.sum((tiles[:, None, :] < tiles[:, :, None]).astype(jnp.int32), axis=2)
    param = jnp.arange(8, dtype=jnp.int32)[None, :]
    rank_own = lax.dynamic_slice_in_dim(rank, device, 1, 0).reshape(scn, 1)
    target = (rank_own // group) * rows + param * group + rank_own % group
    target = jnp.where(param < 6, target, -1).reshape(1, scn * 8)
    wanted = jnp.arange(group, dtype=jnp.int32) + row_index * group
    held = jnp.sum(jnp.where(rank[:, None, :] == wanted[None, :, None], tiles[:, None, :], 0), axis=2)
    held = held - row_index * tile_rows
    place = held[:, None, :] + (jnp.arange(6, dtype=jnp.int32) * tile_rows)[None, :, None]
    place = place.reshape(devices, 6 * group)
    place = jnp.pad(place, ((0, 0), (0, rows - 6 * group)), constant_values=-1).reshape(1, devices * rows)
    map_row = tile_map.reshape(1, scenes)

    vmem = pl.BlockSpec(memory_space=pltpu.VMEM)
    f32 = jnp.float32
    mat, diag, grad, panel = pl.pallas_call(
        functools.partial(assemble_kernel, nrow, ncol),
        out_shape=(
            jax.ShapeDtypeStruct((scn * 8, 6 * scenes), f32),
            jax.ShapeDtypeStruct((48, scenes), f32),
            jax.ShapeDtypeStruct((8, scenes), f32),
            jax.ShapeDtypeStruct((devices, rows, 6 * width), jnp.bfloat16),
        ),
        in_specs=[vmem] * 7,
        out_specs=(vmem,) * 4,
        scratch_shapes=[
            pltpu.VMEM((points // LANES * scn * ROWS, LANES), f32),
            pltpu.VMEM((scn, points), jnp.int32),
            pltpu.VMEM((OTHER_ROWS, scenes), f32),
        ],
        compiler_params=pltpu.CompilerParams(vmem_limit_bytes=VMEM_LIMIT),
        name="assemble",
    )(cam_jac, pt_jac, resid, partner, count.reshape(scn, 1), map_row, target)

    turns = ITERS + 1
    dma = pltpu.SemaphoreType.DMA
    recv, sol, res = pl.pallas_call(
        functools.partial(iterate_kernel, nrow, ncol, scn),
        out_shape=(
            jax.ShapeDtypeStruct((devices, rows, 6 * width), jnp.bfloat16),
            jax.ShapeDtypeStruct((8, scenes), f32),
            jax.ShapeDtypeStruct((8, scenes), f32),
        ),
        in_specs=[vmem] * 4,
        out_specs=(vmem,) * 3,
        scratch_shapes=[
            pltpu.VMEM((turns, ncol, 8, scenes), f32),
            pltpu.VMEM((turns, nrow, 8, scenes), f32),
            dma((devices,)),
            dma((devices,)),
            dma((turns, ncol)),
            dma((turns, ncol)),
            dma((turns, nrow)),
            dma((turns, nrow)),
        ],
        compiler_params=pltpu.CompilerParams(
            collective_id=0, has_side_effects=True, vmem_limit_bytes=VMEM_LIMIT
        ),
        name="iterate",
    )(mat, diag, grad, panel)

    return pl.pallas_call(
        place_kernel,
        out_shape=(
            jax.ShapeDtypeStruct((6, 6, tile_rows, width), jnp.bfloat16),
            jax.ShapeDtypeStruct((6, tile_rows), f32),
            jax.ShapeDtypeStruct((6, tile_rows), f32),
        ),
        in_specs=[vmem] * 5,
        out_specs=(vmem,) * 3,
        compiler_params=pltpu.CompilerParams(vmem_limit_bytes=VMEM_LIMIT),
        name="place",
    )(recv.reshape(devices * rows, 6 * width), place, map_row, sol, res)


def solution(mesh):
    return jax.shard_map(
        shards,
        mesh=mesh,
        in_specs=(
            P(None, None, None, ("row", "col"), None),
            P(None, None, None, ("row", "col"), None),
            P(None, None, ("row", "col"), None),
            P(("row", "col"), None),
            P(("row", "col")),
            P(),
        ),
        out_specs=(P(None, None, "row", "col"), P(None, "row"), P(None, "row")),
        check_vma=False,
    )
```

time: 398 us -> 80.9 us (0.20)
  blocking collectives: 162 us -> 0 us
  Pallas kernels: 0 us -> 73.6 us
  waiting for transfers between devices: 71.8 us -> 0 us
  local copies, waits for them, and re-layouts: 53.9 us -> 5.96 us
  other arithmetic: 44.9 us -> 0.32 us
  matrix products: 33.6 us -> 0 us
  between operations: 21.2 us -> 0.7 us
  starting transfers between devices: 7.36 us -> 0 us
    psum x4 -> x0, blocking collectives: 162 us -> none  [the longest x3 121 us: tile_products(): return lax.psum(spread, ('row', 'col'))]
    pallas_call x0 -> x3, Pallas kernels: none -> 73.6 us  [the longest x1 51.5 us: shards(): pl.pallas_call(functools.partial(iterate_kernel, nrow, ncol, scn), out_sh...]
    psum x1 -> x0, waiting for transfers between devices: 71.8 us -> none  [shards(): diag_all, grad_all = lax.psum((diag_part, grad_part), ('row', 'col'))]
    dynamic_slice x39 -> x1, local copies, waits for them, and re-layouts: 44.8 us -> 0.18 us  [shards(): rank_own = lax.dynamic_slice_in_dim(rank, device, 1, 0).reshape(scn, 1)]
    dot_general x25 -> x0, matrix products: 33.6 us -> none  [the longest x16 26.2 us: scene_sums(): jnp.dot(scene_values, onehot, precision=lax.Precision.HIGHEST, preferred_...]
    reduce_sum x35 -> x2, other arithmetic: 28.8 us -> 0.13 us  [the longest x1 0.09 us: shards(): jnp.sum(jnp.where(rank[:, None, :] == wanted[None, :, None], tiles[:, Non...]
    all_to_all x1 -> x0, starting transfers between devices: 7.32 us -> none  [shards(): lax.all_to_all(shaped, ('row', 'col'), split_axis=1, concat_axis=1, tiled...]
    unnamed x28 -> x0, local copies, waits for them, and re-layouts: 4.99 us -> none
  transfers between devices with their start and end apart: 2 -> 0, of which waited for: 1 -> 0; matrix products, arithmetic and copies ran while one was open for 2% -> 0% of each run, Pallas kernels for 0% -> 0%
where the time goes in v1:
time: 80.9 us; the launch traced here: 80.6 us
  Pallas kernels  73.6 us (91%)
  local copies, waits for them, and re-layouts  5.96 us (7%)
    pallas_call x1, Pallas kernels, shards(): pl.pallas_call(functools.partial(iterate_kernel, nrow, ncol, scn), out_sh...  51.5 us
    pallas_call x1, Pallas kernels, shards(): pl.pallas_call(functools.partial(assemble_kernel, nrow, ncol), out_shape=...  19.2 us
    pallas_call x1, Pallas kernels, shards(): pl.pallas_call(place_kernel, out_shape=(jax.ShapeDtypeStruct((6, 6, tile_...  2.95 us
    pallas_call x1, local copies, waits for them, and re-layouts, shards(): pl.pallas_call(place_kernel, out_shape=(jax.ShapeDtypeStruct((6, 6, tile_...  2.23 us

profile of v1, /device:TPU:0, one launch (start us, length us, event | category | flops | bytes accessed | tf_op | source)
XLA Modules:
  0.0 80.6 jit_solution(1077348121772938014)
XLA Ops:
  0.7 1.3 %copy.21.count_ref = s32[16,1]{1,0:T(8,128)} copy(s32[16,1]{0,1:T(1,128)} %bitcast.6) | data formatting | bytes 128 | tf_op jit(solution)/shard_map/reshape | solution.py:358
  2.0 0.8 lt.33
  2.8 0.1 copy.19
  2.9 0.1 select_reduce_fusion
  3.0 0.2 dynamic-slice_reduce_fusion
  3.2 0.1 add_select_fusion
  3.3 0.6 select_n.47.target_ref
  3.9 0.1 copy.23
  4.0 0.1 broadcast_add_fusion
  4.0 0.7 add.106.place_ref
  4.7 19.2 %assemble.1 = (f32[128,3072]{1,0:T(8,128)}, f32[48,512]{1,0:T(8,128)}, f32[8,512]{1,0:T(8,128)}, bf16[32,24,384]{2,1,0:T(8,128)(2,1)}) custom-call(bf16[2,2,6,16,1024]{4,3,2,1,0:T(8,128)(2,1)} %cam_ref.1, bf16[2,2,3,16,1024]{4,3,2,1,0:T(8,128)(2,1)} %pt_ref.1, bf16[2,2,16,1024]{3,2,1,0:T(8,128)(2,1)} %err_ref.1, s32[16,1024]{1,0:T(8,128)} %partner_ref.1, ...), custom_call_target="tpu_custom_call" | custom-call | tf_op jit(solution)/shard_map/assemble/pallas_call | solution.py:341
  23.9 51.5 %iterate.1 = (bf16[32,24,384]{2,1,0:T(8,128)(2,1)}, f32[8,512]{1,0:T(8,128)}, f32[8,512]{1,0:T(8,128)}) custom-call(f32[128,3072]{1,0:T(8,128)} %get-tuple-element.10.mat_ref, f32[48,512]{1,0:T(8,128)} %get-tuple-element.11.diag_ref, f32[8,512]{1,0:T(8,128)} %get-tuple-element.12.grad_ref, bf16[32,24,384]{2,1,0:T(8,128)(2,1)} %get-tuple-element.13.panel_ref), custom_call_target="tpu_custom_call" | custom-call | tf_op jit(solution)/shard_map/iterate/pallas_call | solution.py:362
  75.4 3.0 %place.1 = (bf16[6,6,128,64]{3,2,1,0:T(8,128)(2,1)}, f32[6,128]{1,0:T(8,128)}, f32[6,128]{1,0:T(8,128)}) custom-call(bf16[768,384]{1,0:T(8,128)(2,1)} %bitcast.3, s32[1,768]{1,0:T(1,128)} %add.106.place_ref, s32[1,512]{1,0:T(1,128)} %bitcast.5, f32[8,512]{1,0:T(8,128)} %get-tuple-element.15.sol_ref, f32[8,512]{1,0:T(8,128)} %get-tuple-element.16.res_ref), custom_call_target="tpu_custom_call" | custom-call | tf_op jit(solution)/shard_map/place/pallas_call | solution.py:387
  78.4 2.2 %copy.24 = bf16[6,6,128,64]{2,3,1,0:T(8,128)(2,1)} copy(bf16[6,6,128,64]{3,2,1,0:T(8,128)(2,1)} %get-tuple-element.26) | data formatting | bytes 1179648 | tf_op jit(solution)/shard_map/place/pallas_call | solution.py:387
  (7 shorter events, 0.1 us)

commit v2 on v1

--- a/solution.py
+++ b/solution.py
@@ -80,8 +80,8 @@
 
 
 def assemble_kernel(
-    nrow, ncol, cam_ref, pt_ref, err_ref, partner_ref, count_ref, map_ref, target_ref,
-    mat_ref, diag_ref, grad_ref, panel_ref, vals, live_partner, acc,
+    nrow, ncol, cam_ref, pt_ref, err_ref, partner_ref, count_ref, map_ref,
+    mat_ref, diag_ref, grad_ref, panel_ref, vals, acc,
 ):
     scn, points = partner_ref.shape
     scenes = map_ref.shape[1]
@@ -94,9 +94,6 @@
         cam = [[[take(cam_ref, s, r, x) for x in range(6)] for r in range(2)] for s in range(2)]
         pt = [[[take(pt_ref, s, r, x) for x in range(3)] for r in range(2)] for s in range(2)]
         err = [[take(err_ref, s, r) for r in range(2)] for s in range(2)]
-        slot = lax.broadcasted_iota(jnp.int32, (scn, LANES), 1) + jb * LANES
-        active = slot < count_ref[...]
-        live_partner[:, lanes] = jnp.where(active, partner_ref[:, lanes], -1)
         link, own, other = point_rows(cam, pt, err)
 
         def put(row, value):
@@ -107,7 +104,7 @@
             put(y * 8 + x, value)
         for u in range(27):
             put(SPARE[u], other[u])
-            put(OTHER_ROWS + u, jnp.where(active, own[u], 0.0))
+            put(OTHER_ROWS + u, own[u])
         put(OTHER_ROWS - 1, zero)
         for u in range(27, OWN_ROWS):
             put(OTHER_ROWS + u, zero)
@@ -117,6 +114,10 @@
     acc[...] = jnp.zeros_like(acc)
     chunk = 256
     low = lax.broadcasted_iota(jnp.int32, (8, chunk), 0) < 6
+
+    spot = lax.broadcasted_iota(jnp.int32, (chunk, points), 0).astype(jnp.float32).astype(jnp.bfloat16)
+    one, nought = jnp.bfloat16(1), jnp.bfloat16(0)
+    slot = lax.broadcasted_iota(jnp.int32, (OWN_ROWS, LANES), 1)
 
     def scene(s, own_sum):
         start = lambda jb: pl.multiple_of((jb * scn + s) * ROWS, 8)
@@ -124,10 +125,12 @@
         high = full.astype(jnp.bfloat16)
         rest = (full - high.astype(jnp.float32)).astype(jnp.bfloat16)
         both = jnp.concatenate([high, rest], axis=0)
-        ids = live_partner[pl.ds(s, 1), :]
+        live = count_ref[s]
+        ids = partner_ref[pl.ds(s, 1), :]
+        ids = jnp.where(lax.broadcasted_iota(jnp.int32, (1, points), 1) < live, ids, -1)
         for b in range(scenes // chunk):
-            spot = lax.broadcasted_iota(jnp.int32, (chunk, points), 0) + b * chunk
-            onehot = jnp.where(spot == ids, 1.0, 0.0).astype(jnp.bfloat16)
+            near = (ids - b * chunk).astype(jnp.float32).astype(jnp.bfloat16)
+            onehot = jnp.where(spot == near, one, nought)
             sums = lax.dot_general(both, onehot, NT, preferred_element_type=jnp.float32)
             sums = sums[:OTHER_ROWS] + sums[OTHER_ROWS:]
             cols = slice(b * chunk, (b + 1) * chunk)
@@ -137,7 +140,12 @@
                 mat_ref[pl.ds(pl.multiple_of(s * 8, 8), 8), y * scenes + b * chunk : y * scenes + (b + 1) * chunk] = (
                     part.astype(jnp.bfloat16).astype(jnp.float32)
                 )
-        own = total_of([vals[pl.ds(start(jb) + OTHER_ROWS, OWN_ROWS), :] for jb in range(blocks)])
+        own = total_of(
+            [
+                jnp.where(slot < live - jb * LANES, vals[pl.ds(start(jb) + OTHER_ROWS, OWN_ROWS), :], 0.0)
+                for jb in range(blocks)
+            ]
+        )
         own = jnp.sum(own, axis=1, keepdims=True)
         here = lax.broadcasted_iota(jnp.int32, (OWN_ROWS, scenes), 1) == base + s
         return own_sum + jnp.where(here, own, 0.0)
@@ -156,9 +164,19 @@
             grad_ref[u - 21 : u - 20, :] = row
 
     rows = panel_ref.shape[1]
+    group = scn // nrow
+    line = lax.broadcasted_iota(jnp.int32, (scn * 8, scenes), 0)
+    lane = lax.broadcasted_iota(jnp.int32, (scn * 8, scenes), 1) - base
+    tiles = map_ref[...]
+    mine = jnp.sum(jnp.where(lane == line // 8, tiles, 0), axis=1, keepdims=True)
+    lower = (lane >= 0) & (lane < scn) & (tiles < mine)
+    rank = jnp.sum(jnp.where(lower, 1, 0), axis=1, keepdims=True)
+    param = line[:, :1] % 8
+    target = (rank // group) * rows + param * group + rank % group
+    target = jnp.where(param < 6, target, -1)
     order = jnp.where(
-        lax.broadcasted_iota(jnp.int32, (nrow * rows, scn * 8), 0) == target_ref[...], 1.0, 0.0
-    ).astype(jnp.bfloat16)
+        lax.broadcasted_iota(jnp.int32, (scn * 8, nrow * rows), 1) == target, 1.0, 0.0
+    ).T.astype(jnp.bfloat16)
     spots = jnp.where(
         lax.broadcasted_iota(jnp.int32, (scenes, scenes), 0) == map_ref[...], 1.0, 0.0
     ).astype(jnp.bfloat16)
@@ -205,7 +223,7 @@
             device_id_type=MESH,
         )
 
-    def gathered(value, buf, spot, turn, size, send, recv, device_of, between=None):
+    def gathered(value, buf, spot, turn, size, send, recv, device_of):
         buf[turn, spot] = value
         copies = []
         for off in range(1, size):
@@ -219,39 +237,37 @@
             )
             copy.start()
             copies.append(copy)
-        if between is not None:
-            between()
         for copy in copies:
             copy.wait()
         return total_of([buf[turn, i] for i in range(size)])
 
-    def all_sum(value, turn, between=None):
-        value = gathered(value, buf_col, col, turn, ncol, send_c, recv_c, lambda p: (row, p), between)
+    def all_sum(value, turn):
+        value = gathered(value, buf_col, col, turn, ncol, send_c, recv_c, lambda p: (row, p))
         return gathered(value, buf_row, row, turn, nrow, send_r, recv_r, lambda p: (p, col))
 
-    def start_panels():
+    def start_panels(turn):
         def step(off, carry):
             panel_copy(off).start()
             return carry
 
-        lax.fori_loop(1, count, step, 0)
-        recv_ref[me] = panel_ref[me]
+        lax.fori_loop(1 + turn * (count - 1) // ITERS, 1 + (turn + 1) * (count - 1) // ITERS, step, 0)
 
     lane = lax.broadcasted_iota(jnp.int32, (8, scenes), 1)
 
     def local_product(vector):
         flat = jnp.concatenate([vector[y : y + 1] for y in range(6)], axis=1)
 
-        def step(s, carry):
-            back, out = carry
-            here = lane == base + s
-            own = jnp.sum(jnp.where(here, vector, 0.0), axis=1, keepdims=True)
-            part = mat_ref[pl.ds(pl.multiple_of(s * 8, 8), 8), :]
-            ahead = jnp.sum(part * flat, axis=1, keepdims=True)
-            return back + part * own, out + jnp.where(here, ahead, 0.0)
-
-        zero = jnp.zeros((8, scenes), jnp.float32)
-        back, out = lax.fori_loop(0, scn, step, (jnp.zeros((8, 6 * scenes), jnp.float32), zero))
+        out = jnp.zeros((8, scenes), jnp.float32)
+        owns, folds = [], []
+        for s in range(scn):
+            owns.append(jnp.sum(jnp.where(lane == base + s, vector, 0.0), axis=1, keepdims=True))
+        back = None
+        for s in range(scn):
+            part = mat_ref[s * 8 : s * 8 + 8, :]
+            folds.append(jnp.sum(part * flat, axis=1, keepdims=True))
+            back = part * owns[s] if back is None else back + part * owns[s]
+        for s in range(scn):
+            out = out + jnp.where(lane == base + s, folds[s], 0.0)
         back = jnp.sum(back, axis=0, keepdims=True)
         for y in range(6):
             out = out + diag_ref[y * 8 : y * 8 + 8, :] * vector[y : y + 1]
@@ -265,11 +281,13 @@
     def inner(first, second):
         return jnp.sum(jnp.sum(first * second, axis=1, keepdims=True), axis=0, keepdims=True)
 
-    remainder = all_sum(grad_ref[...], 0, start_panels)
+    remainder = all_sum(grad_ref[...], 0)
+    recv_ref[me] = panel_ref[me]
     result = jnp.zeros_like(remainder)
     direction = remainder
     norm_now = inner(remainder, remainder)
     for turn in range(ITERS):
+        start_panels(turn)
         image = CAMERA_DAMPING * direction + all_sum(local_product(direction), turn + 1)
         size = norm_now / inner(direction, image)
         result = result + size * direction
@@ -287,18 +305,25 @@
     lax.fori_loop(1, count, finish, 0)
 
 
-def place_kernel(recv_ref, place_ref, map_ref, sol_ref, res_ref, coupling_ref, update_ref, residual_ref):
-    tile_rows, width = coupling_ref.shape[2:]
+def place_kernel(rows, scn, recv_ref, map_ref, sol_ref, res_ref, coupling_ref, update_ref, residual_ref):
+    width, tile_rows = coupling_ref.shape[2:]
     held = recv_ref.shape[0]
+    scenes = map_ref.shape[1]
+    group = scn * tile_rows // scenes
+    first = lax.axis_index("row") * tile_rows
+    tiles = map_ref[...]
+    place = lax.broadcasted_iota(jnp.int32, (tile_rows, scenes), 0) + first
+    lane = lax.broadcasted_iota(jnp.int32, (tile_rows, scenes), 1)
+    source = jnp.sum(jnp.where(tiles == place, lane // scn, 0), axis=1, keepdims=True)
+    lower = (lane // scn == source) & (tiles >= first) & (tiles < place)
+    spot = source * rows + jnp.sum(jnp.where(lower, 1, 0), axis=1, keepdims=True)
+    flipped = recv_ref[...].T
     for x in range(6):
-        spot = lax.broadcasted_iota(jnp.int32, (tile_rows, held), 0) + x * tile_rows
-        chosen = jnp.where(spot == place_ref[...], 1.0, 0.0).astype(jnp.bfloat16)
-        block = jnp.dot(chosen, recv_ref[...], preferred_element_type=jnp.float32).astype(jnp.bfloat16)
-        for y in range(6):
-            coupling_ref[x, y] = block[:, y * width : (y + 1) * width]
-    scenes = map_ref.shape[1]
-    spot = lax.broadcasted_iota(jnp.int32, (tile_rows, scenes), 0) + lax.axis_index("row") * tile_rows
-    chosen = jnp.where(spot == map_ref[...], 1.0, 0.0).astype(jnp.bfloat16)
+        index = lax.broadcasted_iota(jnp.int32, (tile_rows, held), 1) - x * group
+        chosen = jnp.where(index == spot, 1.0, 0.0).astype(jnp.bfloat16)
+        block = lax.dot_general(flipped, chosen, NT, preferred_element_type=jnp.float32)
+        coupling_ref[x] = block.astype(jnp.bfloat16).reshape(6, width, tile_rows)
+    chosen = jnp.where(tiles == place, 1.0, 0.0).astype(jnp.bfloat16)
     for source, target in ((sol_ref, update_ref), (res_ref, residual_ref)):
         left = source[...]
         moved = None
@@ -320,20 +345,6 @@
     width = scenes // ncol
     group = scn // nrow
     rows = -(-6 * group // 8) * 8
-    row_index = lax.axis_index("row")
-    device = row_index * ncol + lax.axis_index("col")
-    tiles = tile_map.reshape(devices, scn)
-    rank = jnp.sum((tiles[:, None, :] < tiles[:, :, None]).astype(jnp.int32), axis=2)
-    param = jnp.arange(8, dtype=jnp.int32)[None, :]
-    rank_own = lax.dynamic_slice_in_dim(rank, device, 1, 0).reshape(scn, 1)
-    target = (rank_own // group) * rows + param * group + rank_own % group
-    target = jnp.where(param < 6, target, -1).reshape(1, scn * 8)
-    wanted = jnp.arange(group, dtype=jnp.int32) + row_index * group
-    held = jnp.sum(jnp.where(rank[:, None, :] == wanted[None, :, None], tiles[:, None, :], 0), axis=2)
-    held = held - row_index * tile_rows
-    place = held[:, None, :] + (jnp.arange(6, dtype=jnp.int32) * tile_rows)[None, :, None]
-    place = place.reshape(devices, 6 * group)
-    place = jnp.pad(place, ((0, 0), (0, rows - 6 * group)), constant_values=-1).reshape(1, devices * rows)
     map_row = tile_map.reshape(1, scenes)
 
     vmem = pl.BlockSpec(memory_space=pltpu.VMEM)
@@ -346,16 +357,15 @@
             jax.ShapeDtypeStruct((8, scenes), f32),
             jax.ShapeDtypeStruct((devices, rows, 6 * width), jnp.bfloat16),
         ),
-        in_specs=[vmem] * 7,
+        in_specs=[vmem] * 4 + [pl.BlockSpec(memory_space=pltpu.SMEM), vmem],
         out_specs=(vmem,) * 4,
         scratch_shapes=[
             pltpu.VMEM((points // LANES * scn * ROWS, LANES), f32),
-            pltpu.VMEM((scn, points), jnp.int32),
             pltpu.VMEM((OTHER_ROWS, scenes), f32),
         ],
         compiler_params=pltpu.CompilerParams(vmem_limit_bytes=VMEM_LIMIT),
         name="assemble",
-    )(cam_jac, pt_jac, resid, partner, count.reshape(scn, 1), map_row, target)
+    )(cam_jac, pt_jac, resid, partner, count, map_row)
 
     turns = ITERS + 1
     dma = pltpu.SemaphoreType.DMA
@@ -384,18 +394,19 @@
         name="iterate",
     )(mat, diag, grad, panel)
 
-    return pl.pallas_call(
-        place_kernel,
+    coupling, update, residual = pl.pallas_call(
+        functools.partial(place_kernel, rows, scn),
         out_shape=(
-            jax.ShapeDtypeStruct((6, 6, tile_rows, width), jnp.bfloat16),
+            jax.ShapeDtypeStruct((6, 6, width, tile_rows), jnp.bfloat16),
             jax.ShapeDtypeStruct((6, tile_rows), f32),
             jax.ShapeDtypeStruct((6, tile_rows), f32),
         ),
-        in_specs=[vmem] * 5,
+        in_specs=[vmem] * 4,
         out_specs=(vmem,) * 3,
         compiler_params=pltpu.CompilerParams(vmem_limit_bytes=VMEM_LIMIT),
         name="place",
-    )(recv.reshape(devices * rows, 6 * width), place, map_row, sol, res)
+    )(recv.reshape(devices * rows, 6 * width), map_row, sol, res)
+    return jnp.swapaxes(coupling, 2, 3), update, residual
 
 
 def solution(mesh):

time: 80.9 us -> 75.2 us (0.930)
  local copies, waits for them, and re-layouts: 5.96 us -> 0 us
    pallas_call x1 -> x0, local copies, waits for them, and re-layouts: 2.23 us -> none  [shards(): pl.pallas_call(place_kernel, out_shape=(jax.ShapeDtypeStruct((6, 6, tile_...]
    reshape x1 -> x0, local copies, waits for them, and re-layouts: 1.33 us -> none  [shards(): count.reshape(scn, 1)]
    pallas_call x1, Pallas kernels: 51.5 us -> 52.6 us  [shards(): pl.pallas_call(functools.partial(iterate_kernel, nrow, ncol, scn), out_sh...]
    lt x2 -> x0, local copies, waits for them, and re-layouts: 0.83 us -> none  [shards(): tiles[:, None, :] < tiles[:, :, None]]
where the time goes in v2:
time: 75.2 us; the launch traced here: 75 us
  Pallas kernels  74.3 us (99%)
    pallas_call x1, Pallas kernels, shards(): pl.pallas_call(functools.partial(iterate_kernel, nrow, ncol, scn), out_sh...  52.6 us
    pallas_call x1, Pallas kernels, shards(): pl.pallas_call(functools.partial(assemble_kernel, nrow, ncol), out_shape=...  18.6 us
    pallas_call x1, Pallas kernels, shards(): pl.pallas_call(functools.partial(place_kernel, rows, scn), out_shape=(jax...  3.19 us

profile of v2, /device:TPU:0, one launch (start us, length us, event | category | flops | bytes accessed | tf_op | source)
XLA Modules:
  0.0 75.0 jit_solution(4175360111901634494)
XLA Ops:
  0.6 18.6 %assemble.1 = (f32[128,3072]{1,0:T(8,128)}, f32[48,512]{1,0:T(8,128)}, f32[8,512]{1,0:T(8,128)}, bf16[32,24,384]{2,1,0:T(8,128)(2,1)}) custom-call(bf16[2,2,6,16,1024]{4,3,2,1,0:T(8,128)(2,1)} %cam_ref.1, bf16[2,2,3,16,1024]{4,3,2,1,0:T(8,128)(2,1)} %pt_ref.1, bf16[2,2,16,1024]{3,2,1,0:T(8,128)(2,1)} %err_ref.1, s32[16,1024]{1,0:T(8,128)} %partner_ref.1, ...), custom_call_target="tpu_custom_call" | custom-call | tf_op jit(solution)/shard_map/assemble/pallas_call | solution.py:352
  19.2 52.6 %iterate.1 = (bf16[32,24,384]{2,1,0:T(8,128)(2,1)}, f32[8,512]{1,0:T(8,128)}, f32[8,512]{1,0:T(8,128)}) custom-call(f32[128,3072]{1,0:T(8,128)} %get-tuple-element.13.mat_ref, f32[48,512]{1,0:T(8,128)} %get-tuple-element.14.diag_ref, f32[8,512]{1,0:T(8,128)} %get-tuple-element.15.grad_ref, bf16[32,24,384]{2,1,0:T(8,128)(2,1)} %get-tuple-element.16.panel_ref), custom_call_target="tpu_custom_call" | custom-call | tf_op jit(solution)/shard_map/iterate/pallas_call | solution.py:372
  71.8 3.2 %place.1 = (bf16[6,6,64,128]{3,2,1,0:T(8,128)(2,1)}, f32[6,128]{1,0:T(8,128)}, f32[6,128]{1,0:T(8,128)}) custom-call(bf16[768,384]{1,0:T(8,128)(2,1)} %bitcast.3, s32[1,512]{1,0:T(1,128)} %bitcast.5, f32[8,512]{1,0:T(8,128)} %get-tuple-element.18.sol_ref, f32[8,512]{1,0:T(8,128)} %get-tuple-element.19.res_ref), custom_call_target="tpu_custom_call" | custom-call | tf_op jit(solution)/shard_map/place/pallas_call | solution.py:397

commit v3 on v2

--- a/solution.py
+++ b/solution.py
@@ -150,7 +150,7 @@
         here = lax.broadcasted_iota(jnp.int32, (OWN_ROWS, scenes), 1) == base + s
         return own_sum + jnp.where(here, own, 0.0)
 
-    own_sum = lax.fori_loop(0, scn, scene, jnp.zeros((OWN_ROWS, scenes), jnp.float32))
+    own_sum = lax.fori_loop(0, scn, scene, jnp.zeros((OWN_ROWS, scenes), jnp.float32), unroll=4)
     diag_ref[...] = jnp.zeros_like(diag_ref)
     grad_ref[...] = jnp.zeros_like(grad_ref)
     for u in range(27):
@@ -223,7 +223,7 @@
             device_id_type=MESH,
         )
 
-    def gathered(value, buf, spot, turn, size, send, recv, device_of):
+    def gathered(value, buf, spot, turn, size, send, recv, device_of, stage):
         buf[turn, spot] = value
         copies = []
         for off in range(1, size):
@@ -237,20 +237,23 @@
             )
             copy.start()
             copies.append(copy)
+        start_panels(stage)
         for copy in copies:
             copy.wait()
         return total_of([buf[turn, i] for i in range(size)])
 
     def all_sum(value, turn):
-        value = gathered(value, buf_col, col, turn, ncol, send_c, recv_c, lambda p: (row, p))
-        return gathered(value, buf_row, row, turn, nrow, send_r, recv_r, lambda p: (p, col))
+        value = gathered(value, buf_col, col, turn, ncol, send_c, recv_c, lambda p: (row, p), 2 * turn)
+        return gathered(value, buf_row, row, turn, nrow, send_r, recv_r, lambda p: (p, col), 2 * turn + 1)
+
+    stages = 2 * (ITERS + 1)
 
     def start_panels(turn):
         def step(off, carry):
             panel_copy(off).start()
             return carry
 
-        lax.fori_loop(1 + turn * (count - 1) // ITERS, 1 + (turn + 1) * (count - 1) // ITERS, step, 0)
+        lax.fori_loop(1 + turn * (count - 1) // stages, 1 + (turn + 1) * (count - 1) // stages, step, 0)
 
     lane = lax.broadcasted_iota(jnp.int32, (8, scenes), 1)
 
@@ -287,7 +290,6 @@
     direction = remainder
     norm_now = inner(remainder, remainder)
     for turn in range(ITERS):
-        start_panels(turn)
         image = CAMERA_DAMPING * direction + all_sum(local_product(direction), turn + 1)
         size = norm_now / inner(direction, image)
         result = result + size * direction

time: 75.2 us -> 66.6 us (0.89)
  Pallas kernels: 74.3 us -> 65.7 us
    pallas_call x1, Pallas kernels: 52.6 us -> 45.8 us  [shards(): pl.pallas_call(functools.partial(iterate_kernel, nrow, ncol, scn), out_sh...]
    pallas_call x1, Pallas kernels: 18.6 us -> 16.7 us  [shards(): pl.pallas_call(functools.partial(assemble_kernel, nrow, ncol), out_shape=...]
where the time goes in v3:
time: 66.6 us; the launch traced here: 66.4 us
  Pallas kernels  65.7 us (99%)
    pallas_call x1, Pallas kernels, shards(): pl.pallas_call(functools.partial(iterate_kernel, nrow, ncol, scn), out_sh...  45.8 us
    pallas_call x1, Pallas kernels, shards(): pl.pallas_call(functools.partial(assemble_kernel, nrow, ncol), out_shape=...  16.7 us
    pallas_call x1, Pallas kernels, shards(): pl.pallas_call(functools.partial(place_kernel, rows, scn), out_shape=(jax...  3.18 us

profile of v3, /device:TPU:0, one launch (start us, length us, event | category | flops | bytes accessed | tf_op | source)
XLA Modules:
  0.0 66.4 jit_solution(703275454981588292)
XLA Ops:
  0.6 16.7 %assemble.1 = (f32[128,3072]{1,0:T(8,128)}, f32[48,512]{1,0:T(8,128)}, f32[8,512]{1,0:T(8,128)}, bf16[32,24,384]{2,1,0:T(8,128)(2,1)}) custom-call(bf16[2,2,6,16,1024]{4,3,2,1,0:T(8,128)(2,1)} %cam_ref.1, bf16[2,2,3,16,1024]{4,3,2,1,0:T(8,128)(2,1)} %pt_ref.1, bf16[2,2,16,1024]{3,2,1,0:T(8,128)(2,1)} %err_ref.1, s32[16,1024]{1,0:T(8,128)} %partner_ref.1, ...), custom_call_target="tpu_custom_call" | custom-call | tf_op jit(solution)/shard_map/assemble/pallas_call | solution.py:354
  17.4 45.8 %iterate.1 = (bf16[32,24,384]{2,1,0:T(8,128)(2,1)}, f32[8,512]{1,0:T(8,128)}, f32[8,512]{1,0:T(8,128)}) custom-call(f32[128,3072]{1,0:T(8,128)} %get-tuple-element.13.mat_ref, f32[48,512]{1,0:T(8,128)} %get-tuple-element.14.diag_ref, f32[8,512]{1,0:T(8,128)} %get-tuple-element.15.grad_ref, bf16[32,24,384]{2,1,0:T(8,128)(2,1)} %get-tuple-element.16.panel_ref), custom_call_target="tpu_custom_call" | custom-call | tf_op jit(solution)/shard_map/iterate/pallas_call | solution.py:374
  63.2 3.2 %place.1 = (bf16[6,6,64,128]{3,2,1,0:T(8,128)(2,1)}, f32[6,128]{1,0:T(8,128)}, f32[6,128]{1,0:T(8,128)}) custom-call(bf16[768,384]{1,0:T(8,128)(2,1)} %bitcast.3, s32[1,512]{1,0:T(1,128)} %bitcast.5, f32[8,512]{1,0:T(8,128)} %get-tuple-element.18.sol_ref, f32[8,512]{1,0:T(8,128)} %get-tuple-element.19.res_ref), custom_call_target="tpu_custom_call" | custom-call | tf_op jit(solution)/shard_map/place/pallas_call | solution.py:399
